TPU v7x, 256 devices: a whole 4x4x8 slice. The times are simulated.
256 devices in a mesh: site: 16 (over z_hi, y, core), blk: 16 (over z_lo, x).
Axes of the slice: x: 4, y: 4, z: 8 (z_hi: 2, z_lo: 4; z = z_hi * 4 + z_lo), core: 2. Of those that a mesh axis runs over, the one named last changes fastest.
Arguments:
- corner: bfloat16 [16, 96, 128, 128], P('site', 'blk')
- bcorner: bfloat16 [2, 16, 96, 128, 128], P(None, 'site', 'blk'), may hold values from -6 to 6
- edge: bfloat16 [16, 96, 128, 2304], P('site', 'blk'), may hold values from -0.5 to 0.5
- bedge: bfloat16 [16, 96, 128, 2304], P('site', 'blk'), may hold values from -0.5 to 0.5
- proj: bfloat16 [16, 96, 2304, 128], P('site', 'blk'), may hold values from -0.125 to 0.125
- joining: int32 [16, 96], P('site'), may hold values from 0 to 95, as said below
- momentum: float32 [1], replicated, may hold values from 0.5 to 2.5
Outputs:
- new_corner: bfloat16 [16, 96, 128, 128], P('site', 'blk')
- new_bcorner: bfloat16 [2, 16, 96, 128, 128], P(None, 'site', 'blk')
- momentum_sum: float32 [2, 96, 128, 128], P(None, 'blk', 'site')
Inputs may be any that keep to these rules, and one draw needn't show every extreme that they name: Each row of joining is a permutation of the 96 slots. The 6 new slots of one blk device take their blocks from the slots of at most 3 blk devices, exactly 2 from each of them.
All inputs are finite; a program needn't handle non-finite values. Where the computation divides by a largest or mean magnitude, that divisor is 1e-20 or more.
Results may differ from a plain program's by a relative error of at most 0.024.
Values may be sent and summed in bfloat16 or wider, within the bound.
A program may use at most 128 MiB of HBM per device.

v0:
```python
import jax
import jax.numpy as jnp
from jax import lax
from jax.sharding import PartitionSpec as P

epsilon = 1e-06


def shifted(block, axis, distance):
    devices = range(lax.axis_size(axis))
    route = [((i - distance) % len(devices), i) for i in devices]
    return lax.ppermute(block, axis, route)


def product(left, right):
    return jnp.einsum("jmn,jnk->jmk", left, right, preferred_element_type=jnp.float32)


def per_device(corner, bcorner, edge, bedge, proj, joining, momentum):
    per_dev = corner.shape[1]
    my_blk = lax.axis_index("blk")
    my_site = lax.axis_index("site")
    left_corner, left_bcorner = shifted((corner, bcorner), "site", 1)
    corner_here = left_corner[0]
    column = edge[0]
    bcolumn = bedge[0]
    project = proj[0]
    enlarged = product(corner_here, column).astype(jnp.bfloat16)
    real_term = product(left_bcorner[0, 0], column)
    imag_term = product(left_bcorner[1, 0], column)
    inserted = product(corner_here, bcolumn)
    angle = momentum[0] * my_site.astype(jnp.float32)
    cosine = jnp.cos(angle)
    sine = jnp.sin(angle)
    excited_re = (cosine * real_term - sine * imag_term + inserted).astype(jnp.bfloat16)
    excited_im = (sine * real_term + cosine * imag_term).astype(jnp.bfloat16)
    projected = jnp.stack(
        [
            product(enlarged, project).astype(jnp.bfloat16),
            product(excited_re, project).astype(jnp.bfloat16),
            product(excited_im, project).astype(jnp.bfloat16),
        ],
        axis=1,
    )
    local_peak = jnp.max(jnp.abs(projected[:, 0].astype(jnp.float32)))
    peak = lax.pmax(local_peak, "blk")
    sources = lax.dynamic_slice_in_dim(joining[0], my_blk * per_dev, per_dev)
    piece = lax.all_gather(projected, "blk", axis=0, tiled=True)
    picks = (sources[:, None] == jnp.arange(piece.shape[0], dtype=jnp.int32)[None, :]).astype(
        jnp.bfloat16
    )
    routed = jnp.einsum("it,txmn->ixmn", picks, piece, preferred_element_type=jnp.float32)
    scaled = routed / (peak + epsilon)
    new_corner = scaled[:, 0].astype(jnp.bfloat16)
    new_b = jnp.stack([scaled[:, 1], scaled[:, 2]], axis=0).astype(jnp.bfloat16)
    summed = lax.psum_scatter(
        new_b.astype(jnp.float32).astype(jnp.bfloat16), "site", scatter_dimension=2, tiled=True
    ).astype(jnp.float32)
    return (new_corner[None], new_b[:, None], summed)


def solution(mesh):
    in_specs = (
        P("site", "blk", None, None),
        P(None, "site", "blk", None, None),
        P("site", "blk", None, None),
        P("site", "blk", None, None),
        P("site", "blk", None, None),
        P("site", None),
        P(),
    )
    out_specs = (
        P("site", "blk", None, None),
        P(None, "site", "blk", None, None),
        P(None, "blk", "site", None),
    )
    return jax.shard_map(
        per_device, mesh=mesh, in_specs=in_specs, out_specs=out_specs, check_vma=False
    )
```

profile of v0, /device:TPU:1, one launch (start us, length us, event | category | flops | bytes accessed | tf_op | source)
XLA Modules:
  0.0 361.1 jit_solution(6874294399947471244)
XLA Ops:
  7.2 0.0 copy-start
  7.2 0.0 all-gather.2.cloned.1.call-start
  7.2 2.8 collective-permute-start
  10.0 0.1 collective-permute-start.1
  10.9 2.0 collective-permute-done
  12.9 0.0 copy-done
  12.9 5.4 %abs_reduce_fusion = (f32[]{:T(128)}, bf16[6,128,128]{2,1,0:T(8,128)(2,1)}) fusion(bf16[1,6,2304,128]{3,2,1,0:T(8,128)(2,1)} %param.11, bf16[1,6,128,2304]{3,2,1,0:T(8,128)(2,1)S(1)} %copy-done, bf16[1,6,128,128]{3,2,1,0:T(8,128)(2,1)} %collective-permute-done), kind=kOutput, calls=%fused_computation.34 | convolution fusion | flops 908132352 | bytes 7471108 | tf_op jit(solution)/shard_map/jmn,jnk->jmk/dot_general | solution.py:16
  18.3 0.0 collective-permute-done.1
  18.3 2.0 fusion.10
  20.3 2.2 fusion.12
  22.5 0.7 copy-done.1
  23.2 2.9 copy-done.2
  26.2 4.0 %fusion.43 = bf16[6,1,128,128]{3,2,0,1:T(8,128)(2,1)} fusion(bf16[1,6,2304,128]{3,2,1,0:T(8,128)(2,1)} %param.11, f32[6,128,2304]{2,1,0:T(8,128)S(1)} %fusion.10, f32[6,128,2304]{2,1,0:T(8,128)S(1)} %fusion.12, f32[]{:T(128)S(6)} %sin.3, f32[]{:T(128)S(6)} %cos.3), kind=kOutput, calls=%fused_computation.26 | convolution fusion | flops 460161024 | bytes 17891336 | tf_op jit(solution)/shard_map/jmn,jnk->jmk/dot_general | solution.py:16
  30.2 10.1 %fusion.38 = bf16[6,1,128,128]{3,2,0,1:T(8,128)(2,1)} fusion(bf16[1,6,2304,128]{3,2,1,0:T(8,128)(2,1)} %param.11, f32[6,128,2304]{2,1,0:T(8,128)} %copy-done.1, f32[6,128,2304]{2,1,0:T(8,128)} %copy-done.2, f32[]{:T(128)S(6)} %sin.3, f32[]{:T(128)S(6)} %cos.3, bf16[1,6,128,2304]{3,2,1,0:T(8,128)(2,1)} %param.10, ...), kind=kOutput, calls=%fused_computation.25 | convolution fusion | flops 914915328 | bytes 21626888 | tf_op jit(solution)/shard_map/jmn,jnk->jmk/dot_general | solution.py:16
  40.3 2.0 pad_maximum_fusion
  42.3 0.0 all-gather.2.cloned.1.call-update
  42.3 0.0 all-reduce.3.cloned.1.call-start
  42.4 0.1 dynamic-slice_bitcast_fusion
  42.5 39.0 %pmax.7 = f32[]{:T(128)} all-reduce(f32[]{:T(128)} %get-tuple-element.14), channel_id=1, replica_groups=mesh['site'=16,'blk'=16] {'blk'}, use_global_device_ids=true, to_apply=%region_1.0 | all-reduce | flops 1 | bytes 8 | tf_op jit(solution)/shard_map/pmax | solution.py:46
  82.2 85.8 %all-gather.2.cloned.1.call-done = bf16[96,3,128,128]{3,2,0,1:T(8,128)(2,1)} async-done(((bf16[6,3,128,128]{3,2,0,1:T(8,128)(2,1)}), bf16[96,3,128,128]{3,2,0,1:T(8,128)(2,1)}) %all-gather.2.cloned.1.call-update) | async-done | bytes 9437200 | tf_op jit(solution)/shard_map/all_gather | solution.py:48
  167.9 8.8 %fusion.46 = bf16[6,3,128,128]{3,0,2,1:T(8,128)(2,1)S(1)} fusion(bf16[96,3,128,128]{3,2,0,1:T(8,128)(2,1)} %all-gather.2.cloned.1.call-done, f32[]{:T(128)S(6)} %add.17, s32[6]{0:T(128)S(1)} %dynamic-slice_bitcast_fusion), kind=kOutput, calls=%fused_computation.27 | convolution fusion | flops 57213504 | bytes 10027036 | tf_op jit(solution)/shard_map/it,txmn->ixmn/dot_general | solution.py:52
  176.7 1.0 fusion.54
  177.7 0.1 pad_maximum_fusion.2
  177.8 1.4 copy.15
  179.2 0.0 all-reduce.3.cloned.1.call-update
  179.2 0.6 dynamic-slice.1
  180.5 1.2 pad_maximum_fusion.1
  181.6 0.8 copy.17
  182.4 1.7 copy.16
  184.1 168.7 %all-reduce.3.cloned.1.call-done = bf16[2,6,128,128]{3,0,1,2:T(2,128)(2,1)} async-done(((bf16[2,6,128,128]{3,0,1,2:T(2,128)(2,1)}), bf16[2,6,128,128]{3,0,1,2:T(2,128)(2,1)}) %all-reduce.3.cloned.1.call-update) | async-done | bytes 393232
  352.8 0.8 dynamic-slice_convert_fusion
  353.6 0.6 copy.18
  (6 shorter events, 0.0 us)
Async XLA Ops:
  7.2 5.8 %copy-start = (bf16[1,6,128,2304]{3,2,1,0:T(8,128)(2,1)S(1)}, bf16[1,6,128,2304]{3,2,1,0:T(8,128)(2,1)}, u32[]{:S(2)}) copy-start(bf16[1,6,128,2304]{3,2,1,0:T(8,128)(2,1)} %param.9) | copy-start | bytes 10616836
  7.2 160.7 %all-gather.2.cloned.1.call-start = ((), (), s32[]{:S(2)}) async-start(), calls=%async_computation | async-start | bytes 10027008 | tf_op jit(solution)/shard_map/all_gather | solution.py:48
  7.2 5.7 %collective-permute-start = (bf16[1,6,128,128]{3,2,1,0:T(8,128)(2,1)}, bf16[1,6,128,128]{3,2,1,0:T(8,128)(2,1)}, u32[]{:S(2)}, u32[]{:S(2)}) collective-permute-start(bf16[1,6,128,128]{3,2,1,0:T(8,128)(2,1)} %param.7), channel_id=1, source_target_pairs={{240,0},{0,16},{16,32},{32,48},{48,64},{64,80},{80,96},{96,112},{1... | collective-permute-start | bytes 589832 | tf_op jit(solution)/shard_map/ppermute | solution.py:12
  10.0 8.3 %collective-permute-start.1 = (bf16[2,1,6,128,128]{4,3,2,1,0:T(8,128)(2,1)}, bf16[2,1,6,128,128]{4,3,2,1,0:T(8,128)(2,1)}, u32[]{:S(2)}, u32[]{:S(2)}) collective-permute-start(bf16[2,1,6,128,128]{4,3,2,1,0:T(8,128)(2,1)} %param.8), channel_id=1, source_target_pairs={{240,0},{0,16},{16,32},{32,48},{48,64},{64,80},{80,96},{96,112},{1... | collective-permute-start | bytes 1179656 | tf_op jit(solution)/shard_map/ppermute | solution.py:12
  20.3 2.9 copy-start.1
  23.2 2.9 copy-start.2
  30.2 12.2 %copy-start.3 = (s32[1,96]{1,0:T(1,128)S(1)}, s32[1,96]{1,0:T(1,128)}, u32[]{:S(2)}) copy-start(s32[1,96]{1,0:T(1,128)} %param.12) | copy-start | bytes 1156
  42.3 310.5 %all-reduce.3.cloned.1.call-start = ((), (), s32[]{:S(2)}) async-start(), calls=%async_computation.1 | async-start | bytes 786432
  176.7 2.5 copy-start.4
Sparse Core Ops, SparseCore 0:
  42.4 125.4 all-gather.1
  179.3 173.4 all-reduce.2
where the time goes:
time: 361 us
  waiting for transfers between devices  257 us (71%)
  blocking collectives  39 us (11%)
  matrix products  32.5 us (9%)
  between operations  16.2 us (4%)
  local copies, waits for them, and re-layouts  9.75 us (3%)
  other arithmetic  4.03 us (1%)
    unnamed x3, waiting for transfers between devices  169 us
    all_gather x1, waiting for transfers between devices, per_device(): piece = lax.all_gather(projected, 'blk', axis=0, tiled=True)  85.8 us
    pmax x1, blocking collectives, per_device(): peak = lax.pmax(local_peak, 'blk')  39 us
    dot_general x5, matrix products, product(): jnp.einsum('jmn,jnk->jmk', left, right, preferred_element_type=jnp.float32)  23.7 us
    dot_general x1, matrix products, per_device(): jnp.einsum('it,txmn->ixmn', picks, piece, preferred_element_type=jnp.floa...  8.79 us
    unnamed x14, local copies, waits for them, and re-layouts  7.33 us
  transfers between devices with their start and end apart: 4, of which 3 were waited for; matrix products, arithmetic and copies ran while one was open for 3% of the time, Pallas kernels for 0%

commit v1 on v0

--- a/solution.py
+++ b/solution.py
@@ -45,7 +45,9 @@
     local_peak = jnp.max(jnp.abs(projected[:, 0].astype(jnp.float32)))
     peak = lax.pmax(local_peak, "blk")
     sources = lax.dynamic_slice_in_dim(joining[0], my_blk * per_dev, per_dev)
-    piece = lax.all_gather(projected, "blk", axis=0, tiled=True)
+    piece = jnp.concatenate(
+        lax.all_to_all(jnp.stack([projected] * lax.axis_size("blk")), "blk", 0, 0), axis=0
+    )
     picks = (sources[:, None] == jnp.arange(piece.shape[0], dtype=jnp.int32)[None, :]).astype(
         jnp.bfloat16
     )

time: 361 us -> 484 us (1.34)
  blocking collectives: 39 us -> 171 us
  waiting for transfers between devices: 257 us -> 233 us
  starting transfers between devices: 2.93 us -> 11.3 us
  local copies, waits for them, and re-layouts: 9.75 us -> 15.8 us
    pmax x1, blocking collectives: 39 us -> 171 us  [per_device(): peak = lax.pmax(local_peak, 'blk')]
    all_gather x1 -> x0, waiting for transfers between devices: 85.8 us -> none  [per_device(): piece = lax.all_gather(projected, 'blk', axis=0, tiled=True)]
    unnamed x3 -> x2, waiting for transfers between devices: 169 us -> 231 us
    all_to_all x0 -> x1, starting transfers between devices: none -> 8.36 us  [per_device(): lax.all_to_all(jnp.stack([projected] * lax.axis_size('blk')), 'blk', 0, 0)]
    another operation x0 -> x2, local copies, waits for them, and re-layouts: none -> 6.08 us  [the longest x1 6.04 us: per_device(): jnp.stack([projected] * lax.axis_size('blk'))]
  transfers between devices with their start and end apart: 4 -> 4, of which waited for: 3 -> 2; matrix products, arithmetic and copies ran while one was open for 3% -> 2% of each run, Pallas kernels for 0% -> 0%
where the time goes in v1:
time: 484 us
  waiting for transfers between devices  233 us (48%)
  blocking collectives  171 us (35%)
  matrix products  32.5 us (7%)
  between operations  16.2 us (3%)
  local copies, waits for them, and re-layouts  15.8 us (3%)
  starting transfers between devices  11.3 us (2%)
    unnamed x2, waiting for transfers between devices  231 us
    pmax x1, blocking collectives, per_device(): peak = lax.pmax(local_peak, 'blk')  171 us
    dot_general x5, matrix products, product(): jnp.einsum('jmn,jnk->jmk', left, right, preferred_element_type=jnp.float32)  23.7 us
  transfers between devices with their start and end apart: 4, of which 2 were waited for; matrix products, arithmetic and copies ran while one was open for 2% of the time, Pallas kernels for 0%

profile of v1, /device:TPU:1, one launch (start us, length us, event | category | flops | bytes accessed | tf_op | source)
XLA Modules:
  0.0 483.6 jit_solution(4408063963492632730)
XLA Ops:
  7.2 0.0 copy-start
  7.2 2.8 collective-permute-start
  9.9 0.1 collective-permute-start.1
  10.8 2.0 collective-permute-done
  12.9 5.4 %abs_reduce_fusion = (f32[]{:T(128)}, bf16[6,128,128]{2,1,0:T(8,128)(2,1)}) fusion(bf16[1,6,2304,128]{3,2,1,0:T(8,128)(2,1)} %param.11, bf16[1,6,128,2304]{3,2,1,0:T(8,128)(2,1)S(1)} %copy-done, bf16[1,6,128,128]{3,2,1,0:T(8,128)(2,1)} %collective-permute-done), kind=kOutput, calls=%fused_computation.34 | convolution fusion | flops 908132352 | bytes 7471108 | tf_op jit(solution)/shard_map/jmn,jnk->jmk/dot_general | solution.py:16
  18.3 0.0 collective-permute-done.1
  18.3 2.0 fusion.10
  20.3 0.0 copy-start.1
  20.3 2.2 fusion.12
  22.5 0.7 copy-done.1
  23.2 2.9 copy-done.2
  26.1 4.0 fusion.43
  30.1 10.1 %fusion.38 = bf16[6,1,128,128]{3,2,0,1:T(8,128)(2,1)} fusion(bf16[1,6,2304,128]{3,2,1,0:T(8,128)(2,1)} %param.11, f32[6,128,2304]{2,1,0:T(8,128)} %copy-done.1, f32[6,128,2304]{2,1,0:T(8,128)} %copy-done.2, f32[]{:T(128)S(6)} %sin.3, f32[]{:T(128)S(6)} %cos.3, bf16[1,6,128,2304]{3,2,1,0:T(8,128)(2,1)} %param.10, ...), kind=kOutput, calls=%fused_computation.25 | convolution fusion | flops 914915328 | bytes 21626888 | tf_op jit(solution)/shard_map/jmn,jnk->jmk/dot_general | solution.py:16
  40.2 1.2 pad_maximum_fusion
  41.5 6.0 %stack.45 = bf16[16,6,3,128,128]{4,3,2,1,0:T(8,128)(2,1)} broadcast(bf16[6,3,128,128]{3,2,1,0:T(8,128)(2,1)S(1)} %copy.19), dimensions={1,2,3,4} | broadcast | bytes 10027008 | tf_op jit(solution)/shard_map/stack | solution.py:49
  47.5 8.4 %all-to-all-start = ((bf16[16,6,3,128,128]{4,3,2,1,0:T(8,128)(2,1)}), bf16[16,6,3,128,128]{4,3,2,1,0:T(8,128)(2,1)}, u32[]{:S(2)}, u32[]{:S(2)}) async-start(bf16[16,6,3,128,128]{4,3,2,1,0:T(8,128)(2,1)} %stack.45), calls=%async_computation | async-start | bytes 18874368 | tf_op jit(solution)/shard_map/all_to_all | solution.py:49
  55.9 0.0 all-reduce.3.cloned.1.call-start
  56.0 0.1 dynamic-slice_bitcast_fusion
  56.0 171.3 %pmax.7 = f32[]{:T(128)} all-reduce(f32[]{:T(128)} %get-tuple-element.17), channel_id=1, replica_groups=mesh['site'=16,'blk'=16] {'blk'}, use_global_device_ids=true, to_apply=%region_1.0 | all-reduce | flops 1 | bytes 8 | tf_op jit(solution)/shard_map/pmax | solution.py:46
  228.0 0.0 all-to-all-done
  228.0 8.8 %fusion.46 = bf16[6,3,128,128]{3,0,2,1:T(8,128)(2,1)S(1)} fusion(bf16[96,3,128,128]{3,2,1,0:T(8,128)(2,1)} %bitcast.13, f32[]{:T(128)S(6)} %add.17, s32[6]{0:T(128)S(1)} %dynamic-slice_bitcast_fusion), kind=kOutput, calls=%fused_computation.27 | convolution fusion | flops 57213504 | bytes 10027036 | tf_op jit(solution)/shard_map/it,txmn->ixmn/dot_general | solution.py:54
  236.8 1.0 fusion.54
  237.7 0.1 pad_maximum_fusion.2
  237.9 1.4 copy.21
  239.2 0.0 all-reduce.3.cloned.1.call-update
  239.3 0.6 dynamic-slice.1
  240.5 1.2 pad_maximum_fusion.1
  241.7 0.8 copy.23
  242.5 1.7 copy.22
  244.1 231.2 %all-reduce.3.cloned.1.call-done = bf16[2,6,128,128]{3,0,1,2:T(2,128)(2,1)} async-done(((bf16[2,6,128,128]{3,0,1,2:T(2,128)(2,1)}), bf16[2,6,128,128]{3,0,1,2:T(2,128)(2,1)}) %all-reduce.3.cloned.1.call-update) | async-done | bytes 393232
  475.4 0.8 dynamic-slice_convert_fusion
  476.1 0.6 copy.24
  (7 shorter events, 0.1 us)
Async XLA Ops:
  7.2 5.7 %copy-start = (bf16[1,6,128,2304]{3,2,1,0:T(8,128)(2,1)S(1)}, bf16[1,6,128,2304]{3,2,1,0:T(8,128)(2,1)}, u32[]{:S(2)}) copy-start(bf16[1,6,128,2304]{3,2,1,0:T(8,128)(2,1)} %param.9) | copy-start | bytes 10616836
  7.2 5.7 %collective-permute-start = (bf16[1,6,128,128]{3,2,1,0:T(8,128)(2,1)}, bf16[1,6,128,128]{3,2,1,0:T(8,128)(2,1)}, u32[]{:S(2)}, u32[]{:S(2)}) collective-permute-start(bf16[1,6,128,128]{3,2,1,0:T(8,128)(2,1)} %param.7), channel_id=1, source_target_pairs={{240,0},{0,16},{16,32},{32,48},{48,64},{64,80},{80,96},{96,112},{1... | collective-permute-start | bytes 589832 | tf_op jit(solution)/shard_map/ppermute | solution.py:12
  9.9 8.3 %collective-permute-start.1 = (bf16[2,1,6,128,128]{4,3,2,1,0:T(8,128)(2,1)}, bf16[2,1,6,128,128]{4,3,2,1,0:T(8,128)(2,1)}, u32[]{:S(2)}, u32[]{:S(2)}) collective-permute-start(bf16[2,1,6,128,128]{4,3,2,1,0:T(8,128)(2,1)} %param.8), channel_id=1, source_target_pairs={{240,0},{0,16},{16,32},{32,48},{48,64},{64,80},{80,96},{96,112},{1... | collective-permute-start | bytes 1179656 | tf_op jit(solution)/shard_map/ppermute | solution.py:12
  20.3 2.9 copy-start.1
  23.2 2.9 copy-start.2
  47.5 8.4 %copy-start.3 = (s32[1,96]{1,0:T(1,128)S(1)}, s32[1,96]{1,0:T(1,128)}, u32[]{:S(2)}) copy-start(s32[1,96]{1,0:T(1,128)} %param.12) | copy-start | bytes 1156
  47.5 180.4 %all-to-all-start = ((bf16[16,6,3,128,128]{4,3,2,1,0:T(8,128)(2,1)}), bf16[16,6,3,128,128]{4,3,2,1,0:T(8,128)(2,1)}, u32[]{:S(2)}, u32[]{:S(2)}) async-start(bf16[16,6,3,128,128]{4,3,2,1,0:T(8,128)(2,1)} %stack.45), calls=%async_computation | async-start | bytes 18874368 | tf_op jit(solution)/shard_map/all_to_all | solution.py:49
  55.9 419.5 %all-reduce.3.cloned.1.call-start = ((), (), s32[]{:S(2)}) async-start(), calls=%async_computation.1 | async-start | bytes 786432
  236.8 2.5 copy-start.4
Sparse Core Ops, SparseCore 0:
  239.4 235.9 all-reduce.2
